TPU v7x, 32 devices: a whole 2x2x4 slice. The times are simulated.
32 devices in a mesh: dp: 32 (over z, y, x, core).
Axes of the slice: x: 2, y: 2, z: 4, core: 2. Of those that a mesh axis runs over, the one named last changes fastest.
Arguments:
- grads: bfloat16 [64, 1024, 1024], P('dp'), may hold values from -6 to 6
- memory: bfloat16 [64, 1024, 1024], P('dp'), may hold values from -6 to 6
- block_ids: int32 [16], replicated, may hold values from 0 to 63, as said below
- layer_ids: int32 [16], replicated, may hold values from 0 to 1, as said below
- master: float32 [128, 16384], P(None, 'dp'), may hold values from -8 to 8
- first_moment: float32 [128, 16384], P(None, 'dp'), may hold values from -8 to 8
- second_moment: float32 [128, 16384], P(None, 'dp'), may hold values from 0.25 to 4
Outputs:
- new_memory: bfloat16 [64, 1024, 1024], P('dp')
- master_new: float32 [128, 16384], P(None, 'dp')
- first_new: float32 [128, 16384], P(None, 'dp')
- second_new: float32 [128, 16384], P(None, 'dp')
- step_blocks: bfloat16 [16, 16384], replicated
Inputs may be any that keep to these rules, and one draw needn't show every extreme that they name: Block ids number the 64 tiles of a layer, and the pairs (layer_ids[k], block_ids[k]) are distinct. `layer_ids`: every layer is named by at least a quarter of the 16 entries, rounded down.
All inputs are finite; a program needn't handle non-finite values.
Results may differ from a plain program's by a relative error of at most 0.0004.
Values may be sent and summed in bfloat16 or wider, within the bound.
A program may use at most 64 MiB of HBM per device.

v0:
```python
import jax
import jax.numpy as jnp
from jax import lax
from jax.sharding import PartitionSpec as P

TILE = 128
filter_rate = 0.3
beta_one = 0.9
beta_two = 0.999
adam_eps = 1e-06
weight_decay = 0.01
learn_rate = 0.01
norm_eps = 1e-06


def take_tiles(source, layer_ids, tile_row, tile_col):

    def single(layer_id, row_tile, col_tile):
        return lax.dynamic_slice(
            source, (layer_id, row_tile * TILE, col_tile * TILE), (1, TILE, TILE)
        )[0]

    return jax.vmap(single)(layer_ids, tile_row, tile_col)


def pack_blocks(grads_dev, memory_dev, layer_ids, tile_row, tile_col):
    grad_tiles = take_tiles(grads_dev, layer_ids, tile_row, tile_col).astype(jnp.float32)
    memory_tiles = take_tiles(memory_dev, layer_ids, tile_row, tile_col).astype(jnp.float32)
    combined = grad_tiles + memory_tiles
    return combined.reshape(combined.shape[0], TILE * TILE)


def selected_mask(layer_ids, block_ids, layers, tile_count):
    columns = layer_ids * (tile_count * tile_count) + block_ids
    all_columns = jnp.arange(layers * tile_count * tile_count, dtype=jnp.int32)
    chosen = jnp.any(columns[:, None] == all_columns[None, :], axis=0)
    return chosen.reshape(layers, tile_count, 1, tile_count, 1)


def filter_memory(grads_dev, memory_dev, chosen):
    layers, model_width, _ = grads_dev.shape
    tile_count = model_width // TILE
    accumulated = grads_dev.astype(jnp.float32) + memory_dev.astype(jnp.float32)
    shaped = accumulated.reshape(layers, tile_count, TILE, tile_count, TILE)
    filtered = jnp.where(chosen, jnp.float32(0.0), shaped).reshape(layers, model_width, model_width)
    mixed = (1.0 - filter_rate) * memory_dev.astype(jnp.float32) + filter_rate * filtered
    return mixed.astype(jnp.bfloat16)


def adam_rows(summed, weights_sel, first_old, second_old):
    first_sel = beta_one * first_old + (1.0 - beta_one) * summed
    second_sel = beta_two * second_old + (1.0 - beta_two) * summed * summed
    update = first_sel / (jnp.sqrt(second_sel) + adam_eps) + weight_decay * weights_sel
    return (first_sel, second_sel, update)


def layer_squares(member, values):
    return jnp.sum(member * jnp.sum(values * values, axis=1)[:, None], axis=0)


def trust_rows(member, weight_total, update_total):
    trust_ratio = jnp.sqrt(weight_total / (update_total + norm_eps))
    return jnp.sum(member * trust_ratio[None, :], axis=1)


def on_device(grads, memory, block_ids, layer_ids, master, first_moment, second_moment):
    layers, model_width, _ = grads.shape
    tile_count = model_width // TILE
    tile_row = block_ids // tile_count
    tile_col = block_ids % tile_count
    columns = layer_ids * (tile_count * tile_count) + block_ids
    member = (layer_ids[:, None] == jnp.arange(layers, dtype=jnp.int32)[None, :]).astype(
        jnp.float32
    )
    weights_sel = jnp.take(master, columns, axis=0)
    first_old = jnp.take(first_moment, columns, axis=0)
    second_old = jnp.take(second_moment, columns, axis=0)
    packed = pack_blocks(grads, memory, layer_ids, tile_row, tile_col)
    summed = lax.psum_scatter(packed, "dp", scatter_dimension=1, tiled=True)
    first_sel, second_sel, update = adam_rows(summed, weights_sel, first_old, second_old)
    weight_total, update_total = lax.psum(
        (layer_squares(member, weights_sel), layer_squares(member, update)), "dp"
    )
    scaled = trust_rows(member, weight_total, update_total)[:, None] * update
    step_blocks = lax.all_gather(scaled.astype(jnp.bfloat16), "dp", axis=1, tiled=True)
    new_memory = filter_memory(
        grads, memory, selected_mask(layer_ids, block_ids, layers, tile_count)
    )
    master_new = master.at[columns].set(weights_sel - learn_rate * scaled)
    first_new = first_moment.at[columns].set(first_sel)
    second_new = second_moment.at[columns].set(second_sel)
    return (new_memory, master_new, first_new, second_new, step_blocks)


def solution(mesh):
    in_specs = (
        P("dp", None, None),
        P("dp", None, None),
        P(),
        P(),
        P(None, "dp"),
        P(None, "dp"),
        P(None, "dp"),
    )
    out_specs = (P("dp", None, None), P(None, "dp"), P(None, "dp"), P(None, "dp"), P())
    return jax.shard_map(
        on_device, mesh=mesh, in_specs=in_specs, out_specs=out_specs, check_vma=False
    )
```

profile of v0, /device:TPU:0, one launch (start us, length us, event | category | flops | bytes accessed | tf_op | source)
XLA Modules:
  0.0 355.8 jit_solution(294397355076881631)
XLA Ops:
  7.2 1.0 copy.36
  8.2 1.0 copy.38
  9.1 0.9 copy.37
  10.9 56.7 %while.3 = (s32[]{:T(128)}, bf16[2,1024,1024]{2,1,0:T(8,128)(2,1)}, s32[16,3]{0,1:T(4,128)S(1)}, bf16[16,1,128,128]{3,2,1,0:T(8,128)(2,1)S(1)}, s32[]{:T(128)}) while((s32[]{:T(128)}, bf16[2,1024,1024]{2,1,0:T(8,128)(2,1)}, s32[16,3]{0,1:T(4,128)S(1)}, bf16[16,1,128,128]{3,2,1,0:T(8,128)(2,1)S(1)}, s32[]{:T(128)}) %tuple.46), condition=%wide.while_cond.1, body=%wide.while_body.1.sunk | while | flops 2 | bytes 65673 | solution.py:19
  11.5 2.9 bitcast_dynamic-update-slice_fusion.5
  15.1 2.9 bitcast_dynamic-update-slice_fusion.5
  18.6 2.9 bitcast_dynamic-update-slice_fusion.5
  22.2 2.9 bitcast_dynamic-update-slice_fusion.5
  25.7 2.9 bitcast_dynamic-update-slice_fusion.5
  29.2 2.9 bitcast_dynamic-update-slice_fusion.5
  32.8 2.9 bitcast_dynamic-update-slice_fusion.5
  36.3 2.9 bitcast_dynamic-update-slice_fusion.5
  39.9 2.9 bitcast_dynamic-update-slice_fusion.5
  43.4 2.9 bitcast_dynamic-update-slice_fusion.5
  47.0 2.9 bitcast_dynamic-update-slice_fusion.5
  50.5 2.9 bitcast_dynamic-update-slice_fusion.5
  54.1 2.9 bitcast_dynamic-update-slice_fusion.5
  57.6 2.9 bitcast_dynamic-update-slice_fusion.5
  61.1 2.9 bitcast_dynamic-update-slice_fusion.5
  64.7 2.9 bitcast_dynamic-update-slice_fusion.5
  67.7 56.7 %while.2 = (s32[]{:T(128)}, bf16[2,1024,1024]{2,1,0:T(8,128)(2,1)}, s32[16,3]{0,1:T(4,128)S(1)}, bf16[16,1,128,128]{3,2,1,0:T(8,128)(2,1)S(1)}, s32[]{:T(128)}) while((s32[]{:T(128)}, bf16[2,1024,1024]{2,1,0:T(8,128)(2,1)}, s32[16,3]{0,1:T(4,128)S(1)}, bf16[16,1,128,128]{3,2,1,0:T(8,128)(2,1)S(1)}, s32[]{:T(128)}) %tuple.56), condition=%wide.while_cond, body=%wide.while_body.sunk | while | flops 2 | bytes 65673 | solution.py:19
  68.3 2.9 bitcast_dynamic-update-slice_fusion.4
  71.9 2.9 bitcast_dynamic-update-slice_fusion.4
  75.4 2.9 bitcast_dynamic-update-slice_fusion.4
  79.0 2.9 bitcast_dynamic-update-slice_fusion.4
  82.5 2.9 bitcast_dynamic-update-slice_fusion.4
  86.1 2.9 bitcast_dynamic-update-slice_fusion.4
  89.6 2.9 bitcast_dynamic-update-slice_fusion.4
  93.2 2.9 bitcast_dynamic-update-slice_fusion.4
  96.7 2.9 bitcast_dynamic-update-slice_fusion.4
  100.2 2.9 bitcast_dynamic-update-slice_fusion.4
  103.8 2.9 bitcast_dynamic-update-slice_fusion.4
  107.3 2.9 bitcast_dynamic-update-slice_fusion.4
  110.9 2.9 bitcast_dynamic-update-slice_fusion.4
  114.4 2.9 bitcast_dynamic-update-slice_fusion.4
  117.9 2.9 bitcast_dynamic-update-slice_fusion.4
  121.5 2.9 bitcast_dynamic-update-slice_fusion.4
  124.6 1.6 copy.14
  126.4 1.9 broadcast_in_dim.51
  128.4 5.3 %broadcast_in_dim.52 = pred[2,1024,1024]{2,1,0:T(8,128)(4,1)S(1)} reshape(pred[2,8,128,8,128]{4,3,2,1,0:T(8,128)(4,1)} %broadcast_in_dim.51) | data formatting | bytes 4194304 | tf_op jit(solution)/shard_map/jit(_where)/broadcast_in_dim | solution.py:45
  135.4 6.2 %fusion.1 = bf16[2,1024,1024]{2,1,0:T(8,128)(2,1)} fusion(bf16[2,1024,1024]{2,1,0:T(8,128)(2,1)} %get-tuple-element.159, pred[2,1024,1024]{2,1,0:T(8,128)(4,1)S(1)} %broadcast_in_dim.52, bf16[2,1024,1024]{2,1,0:T(8,128)(2,1)} %get-tuple-element.160), kind=kLoop, calls=%fused_computation.13 | loop fusion | flops 16777216 | bytes 14680064 | tf_op jit(solution)/shard_map/convert_element_type | solution.py:47
  141.6 124.0 %reduce-scatter.2.cloned.1.call-done = f32[16,512]{1,0:T(8,128)} async-done(((f32[16,16384]{1,0:T(8,128)}), f32[16,512]{1,0:T(8,128)}) %reduce-scatter.2.cloned.1.call-update) | async-done | bytes 32784 | tf_op jit(solution)/shard_map/reduce_scatter | solution.py:79
  265.6 1.0 multiply_reduce_fusion
  266.7 36.9 %all-reduce = (f32[2]{0:T(128)S(1)}, f32[2]{0:T(128)S(1)}) all-reduce(f32[2]{0:T(128)S(1)} %get-tuple-element.23, f32[2]{0:T(128)S(1)} %get-tuple-element.22), channel_id=1, replica_groups=mesh['dp'=32] {'dp'}, use_global_device_ids=true, to_apply=%region_3.5 | all-reduce | flops 4 | bytes 32 | tf_op jit(solution)/shard_map/psum | solution.py:81
  303.7 41.3 %all_gather.3 = bf16[16,16384]{1,0:T(8,128)(2,1)S(1)} all-gather(bf16[16,512]{1,0:T(8,128)(2,1)S(1)} %multiply_convert_fusion), channel_id=1, replica_groups=mesh['dp'=32] {'dp'}, dimensions={1}, use_global_device_ids=true | all-gather | bytes 540672 | tf_op jit(solution)/shard_map/all_gather | solution.py:85
  345.9 1.1 scatter_custom_fusion.1
  347.0 1.1 scatter_custom_fusion.2
  348.1 0.8 copy.40
  (94 shorter events, 23.3 us)
Async XLA Ops:
  7.2 258.4 %reduce-scatter.2.cloned.1.call-start = ((), (), s32[]{:S(2)}) async-start(), calls=%async_computation.1 | async-start | bytes 1081344 | tf_op jit(solution)/shard_map/reduce_scatter | solution.py:79
  8.2 118.0 %copy-start.3 = (s32[16]{0:T(128)S(1)}, s32[16]{0:T(128)}, u32[]{:S(2)}) copy-start(s32[16]{0:T(128)} %param.12) | copy-start | bytes 196
  8.2 118.0 %copy-start.4 = (s32[16]{0:T(128)S(1)}, s32[16]{0:T(128)}, u32[]{:S(2)}) copy-start(s32[16]{0:T(128)} %param.11) | copy-start | bytes 196
  345.8 3.1 copy-start.2
  347.0 2.0 copy-start.1
  348.1 0.9 copy-start
Sparse Core Ops, SparseCore 0:
  126.3 139.2 reduce-scatter.1
where the time goes:
time: 359 us; the launch traced here: 356 us
  local copies, waits for them, and re-layouts  127 us (35%)
  waiting for transfers between devices  124 us (35%)
  blocking collectives  78.1 us (22%)
  between operations  14.2 us (4%)
  other arithmetic  11.5 us (3%)
    reduce_scatter x1, waiting for transfers between devices, on_device(): summed = lax.psum_scatter(packed, 'dp', scatter_dimension=1, tiled=True)  124 us
    gather x96, local copies, waits for them, and re-layouts  113 us
    all_gather x1, blocking collectives, on_device(): lax.all_gather(scaled.astype(jnp.bfloat16), 'dp', axis=1, tiled=True)  41.3 us
    psum x1, blocking collectives, on_device(): lax.psum((layer_squares(member, weights_sel), layer_squares(member, updat...  36.9 us
    broadcast_in_dim x3, local copies, waits for them, and re-layouts, filter_memory(): jnp.where(chosen, jnp.float32(0.0), shaped)  7.3 us
  transfers between devices with their start and end apart: 1, of which 1 were waited for; matrix products, arithmetic and copies ran while one was open for 4% of the time, Pallas kernels for 0%

commit v1 on v0

--- a/solution.py
+++ b/solution.py
@@ -11,6 +11,18 @@
 weight_decay = 0.01
 learn_rate = 0.01
 norm_eps = 1e-06
+
+
+def gather_by_bits(value, axis, dim):
+    ways, here = (lax.axis_size(axis), lax.axis_index(axis))
+    grown, reach = (value, 1)
+    while reach < ways:
+        theirs = lax.ppermute(grown, axis, [(d, d ^ reach) for d in range(ways)])
+        mine_first = jnp.concatenate([grown, theirs], axis=dim)
+        theirs_first = jnp.concatenate([theirs, grown], axis=dim)
+        grown = jnp.where(here & reach == 0, mine_first, theirs_first)
+        reach = 2 * reach
+    return grown
 
 
 def take_tiles(source, layer_ids, tile_row, tile_col):
@@ -82,7 +94,7 @@
         (layer_squares(member, weights_sel), layer_squares(member, update)), "dp"
     )
     scaled = trust_rows(member, weight_total, update_total)[:, None] * update
-    step_blocks = lax.all_gather(scaled.astype(jnp.bfloat16), "dp", axis=1, tiled=True)
+    step_blocks = gather_by_bits(scaled.astype(jnp.bfloat16), "dp", 1)
     new_memory = filter_memory(
         grads, memory, selected_mask(layer_ids, block_ids, layers, tile_count)
     )

time: 359 us -> 348 us (0.969)
  blocking collectives: 78.1 us -> 36.8 us
  waiting for transfers between devices: 124 us -> 146 us
  starting transfers between devices: 0.04 us -> 7.56 us
    all_gather x1 -> x0, blocking collectives: 41.3 us -> none  [on_device(): lax.all_gather(scaled.astype(jnp.bfloat16), 'dp', axis=1, tiled=True)]
    reduce_scatter x1, waiting for transfers between devices: 124 us -> 138 us  [on_device(): summed = lax.psum_scatter(packed, 'dp', scatter_dimension=1, tiled=True)]
    ppermute x0 -> x5, waiting for transfers between devices: none -> 8.78 us  [gather_by_bits(): theirs = lax.ppermute(grown, axis, [(d, d ^ reach) for d in range(ways)])]
    ppermute x0 -> x5, starting transfers between devices: none -> 7.52 us  [gather_by_bits(): theirs = lax.ppermute(grown, axis, [(d, d ^ reach) for d in range(ways)])]
  transfers between devices with their start and end apart: 1 -> 6, of which waited for: 1 -> 5; matrix products, arithmetic and copies ran while one was open for 4% -> 5% of each run, Pallas kernels for 0% -> 0%
where the time goes in v1:
time: 348 us; the launch traced here: 345 us
  waiting for transfers between devices  146 us (42%)
  local copies, waits for them, and re-layouts  127 us (36%)
  blocking collectives  36.8 us (11%)
  between operations  14.3 us (4%)
  other arithmetic  13.1 us (4%)
  starting transfers between devices  7.56 us (2%)
    reduce_scatter x1, waiting for transfers between devices, on_device(): summed = lax.psum_scatter(packed, 'dp', scatter_dimension=1, tiled=True)  138 us
    gather x96, local copies, waits for them, and re-layouts  113 us
    psum x1, blocking collectives, on_device(): lax.psum((layer_squares(member, weights_sel), layer_squares(member, updat...  36.8 us
    ppermute x5, waiting for transfers between devices, gather_by_bits(): theirs = lax.ppermute(grown, axis, [(d, d ^ reach) for d in range(ways)])  8.78 us
    ppermute x5, starting transfers between devices, gather_by_bits(): theirs = lax.ppermute(grown, axis, [(d, d ^ reach) for d in range(ways)])  7.52 us
    broadcast_in_dim x3, local copies, waits for them, and re-layouts, filter_memory(): jnp.where(chosen, jnp.float32(0.0), shaped)  7.3 us
  transfers between devices with their start and end apart: 6, of which 5 were waited for; matrix products, arithmetic and copies ran while one was open for 5% of the time, Pallas kernels for 0%

profile of v1, /device:TPU:0, one launch (start us, length us, event | category | flops | bytes accessed | tf_op | source)
XLA Modules:
  0.0 345.2 jit_solution(7715080315815968605)
XLA Ops:
  10.9 56.7 %while.3 = (s32[]{:T(128)}, bf16[2,1024,1024]{2,1,0:T(8,128)(2,1)}, s32[16,3]{0,1:T(4,128)S(1)}, bf16[16,1,128,128]{3,2,1,0:T(8,128)(2,1)S(1)}, s32[]{:T(128)}) while((s32[]{:T(128)}, bf16[2,1024,1024]{2,1,0:T(8,128)(2,1)}, s32[16,3]{0,1:T(4,128)S(1)}, bf16[16,1,128,128]{3,2,1,0:T(8,128)(2,1)S(1)}, s32[]{:T(128)}) %tuple.46), condition=%wide.while_cond.1, body=%wide.while_body.1.sunk | while | flops 2 | bytes 65673 | solution.py:31
  11.5 2.9 bitcast_dynamic-update-slice_fusion.5
  15.1 2.9 bitcast_dynamic-update-slice_fusion.5
  18.6 2.9 bitcast_dynamic-update-slice_fusion.5
  22.2 2.9 bitcast_dynamic-update-slice_fusion.5
  25.7 2.9 bitcast_dynamic-update-slice_fusion.5
  29.2 2.9 bitcast_dynamic-update-slice_fusion.5
  32.8 2.9 bitcast_dynamic-update-slice_fusion.5
  36.3 2.9 bitcast_dynamic-update-slice_fusion.5
  39.9 2.9 bitcast_dynamic-update-slice_fusion.5
  43.4 2.9 bitcast_dynamic-update-slice_fusion.5
  47.0 2.9 bitcast_dynamic-update-slice_fusion.5
  50.5 2.9 bitcast_dynamic-update-slice_fusion.5
  54.1 2.9 bitcast_dynamic-update-slice_fusion.5
  57.6 2.9 bitcast_dynamic-update-slice_fusion.5
  61.1 2.9 bitcast_dynamic-update-slice_fusion.5
  64.7 2.9 bitcast_dynamic-update-slice_fusion.5
  67.7 56.7 %while.2 = (s32[]{:T(128)}, bf16[2,1024,1024]{2,1,0:T(8,128)(2,1)}, s32[16,3]{0,1:T(4,128)S(1)}, bf16[16,1,128,128]{3,2,1,0:T(8,128)(2,1)S(1)}, s32[]{:T(128)}) while((s32[]{:T(128)}, bf16[2,1024,1024]{2,1,0:T(8,128)(2,1)}, s32[16,3]{0,1:T(4,128)S(1)}, bf16[16,1,128,128]{3,2,1,0:T(8,128)(2,1)S(1)}, s32[]{:T(128)}) %tuple.54), condition=%wide.while_cond, body=%wide.while_body.sunk | while | flops 2 | bytes 65673 | solution.py:31
  68.3 2.9 bitcast_dynamic-update-slice_fusion.4
  71.9 2.9 bitcast_dynamic-update-slice_fusion.4
  75.4 2.9 bitcast_dynamic-update-slice_fusion.4
  79.0 2.9 bitcast_dynamic-update-slice_fusion.4
  82.5 2.9 bitcast_dynamic-update-slice_fusion.4
  86.1 2.9 bitcast_dynamic-update-slice_fusion.4
  89.6 2.9 bitcast_dynamic-update-slice_fusion.4
  93.2 2.9 bitcast_dynamic-update-slice_fusion.4
  96.7 2.9 bitcast_dynamic-update-slice_fusion.4
  100.2 2.9 bitcast_dynamic-update-slice_fusion.4
  103.8 2.9 bitcast_dynamic-update-slice_fusion.4
  107.3 2.9 bitcast_dynamic-update-slice_fusion.4
  110.9 2.9 bitcast_dynamic-update-slice_fusion.4
  114.4 2.9 bitcast_dynamic-update-slice_fusion.4
  117.9 2.9 bitcast_dynamic-update-slice_fusion.4
  121.5 2.9 bitcast_dynamic-update-slice_fusion.4
  124.6 1.6 copy.14
  128.0 137.6 %reduce-scatter.2.cloned.1.call-done = f32[16,512]{1,0:T(8,128)} async-done(((f32[16,16384]{1,0:T(8,128)}), f32[16,512]{1,0:T(8,128)}) %reduce-scatter.2.cloned.1.call-update) | async-done | bytes 32784 | tf_op jit(solution)/shard_map/reduce_scatter | solution.py:91
  266.7 36.8 %all-reduce = (f32[2]{0:T(128)S(1)}, f32[2]{0:T(128)S(1)}) all-reduce(f32[2]{0:T(128)S(1)} %get-tuple-element.23, f32[2]{0:T(128)S(1)} %get-tuple-element.22), channel_id=1, replica_groups=mesh['dp'=32] {'dp'}, use_global_device_ids=true, to_apply=%region_3.5 | all-reduce | flops 4 | bytes 32 | tf_op jit(solution)/shard_map/psum | solution.py:93
  303.7 1.2 collective-permute-done
  304.9 2.3 collective-permute-start.1
  307.2 1.9 collective-permute-done.1
  309.2 2.1 collective-permute-start.2
  311.2 2.3 collective-permute-done.2
  313.5 2.9 collective-permute-start.3
  316.6 1.9 broadcast_in_dim.51
  318.6 5.3 %broadcast_in_dim.52 = pred[2,1024,1024]{2,1,0:T(8,128)(4,1)S(1)} reshape(pred[2,8,128,8,128]{4,3,2,1,0:T(8,128)(4,1)} %broadcast_in_dim.51) | data formatting | bytes 4194304 | tf_op jit(solution)/shard_map/jit(_where)/broadcast_in_dim | solution.py:57
  324.1 6.2 %fusion.1 = bf16[2,1024,1024]{2,1,0:T(8,128)(2,1)} fusion(bf16[2,1024,1024]{2,1,0:T(8,128)(2,1)} %get-tuple-element.149, pred[2,1024,1024]{2,1,0:T(8,128)(4,1)S(1)} %broadcast_in_dim.52, bf16[2,1024,1024]{2,1,0:T(8,128)(2,1)} %get-tuple-element.150), kind=kLoop, calls=%fused_computation.13 | loop fusion | flops 16777216 | bytes 14680064 | tf_op jit(solution)/shard_map/convert_element_type | solution.py:59
  333.0 3.5 %collective-permute-done.4 = bf16[16,8192]{1,0:T(8,128)(2,1)} collective-permute-done((bf16[16,8192]{1,0:T(8,128)(2,1)S(1)}, bf16[16,8192]{1,0:T(8,128)(2,1)}, u32[]{:S(2)}, u32[]{:S(2)}) %collective-permute-start.4) | collective-permute-done | bytes 262176 | tf_op jit(solution)/shard_map/ppermute | solution.py:20
  336.4 1.9 maximum_select_fusion
  (109 shorter events, 29.2 us)
Async XLA Ops:
  7.2 258.4 %reduce-scatter.2.cloned.1.call-start = ((), (), s32[]{:S(2)}) async-start(), calls=%async_computation.1 | async-start | bytes 1081344 | tf_op jit(solution)/shard_map/reduce_scatter | solution.py:91
  8.2 118.0 %copy-start.4 = (s32[16]{0:T(128)S(1)}, s32[16]{0:T(128)}, u32[]{:S(2)}) copy-start(s32[16]{0:T(128)} %param.12) | copy-start | bytes 196
  8.2 118.0 %copy-start.5 = (s32[16]{0:T(128)S(1)}, s32[16]{0:T(128)}, u32[]{:S(2)}) copy-start(s32[16]{0:T(128)} %param.11) | copy-start | bytes 196
  303.7 1.2 collective-permute-start
  304.9 4.2 %collective-permute-start.1 = (bf16[16,1024]{1,0:T(8,128)(2,1)S(1)}, bf16[16,1024]{1,0:T(8,128)(2,1)S(1)}, u32[]{:S(2)}, u32[]{:S(2)}) collective-permute-start(bf16[16,1024]{1,0:T(8,128)(2,1)S(1)} %maximum_select_fusion.4), channel_id=1, source_target_pairs={{0,2},{1,3},{2,0},{3,1},{4,6},{5,7},{6,4},{7,5},{8,10},{9,11},{10,... | collective-permute-start | bytes 98312 | tf_op jit(solution)/shard_map/ppermute | solution.py:20
  309.2 4.3 %collective-permute-start.2 = (bf16[16,2048]{1,0:T(8,128)(2,1)S(1)}, bf16[16,2048]{1,0:T(8,128)(2,1)S(1)}, u32[]{:S(2)}, u32[]{:S(2)}) collective-permute-start(bf16[16,2048]{1,0:T(8,128)(2,1)S(1)} %maximum_select_fusion.3), channel_id=1, source_target_pairs={{0,4},{1,5},{2,6},{3,7},{4,0},{5,1},{6,2},{7,3},{8,12},{9,13},{10,... | collective-permute-start | bytes 196616 | tf_op jit(solution)/shard_map/ppermute | solution.py:20
  313.5 10.3 %collective-permute-start.3 = (bf16[16,4096]{1,0:T(8,128)(2,1)S(1)}, bf16[16,4096]{1,0:T(8,128)(2,1)S(1)}, u32[]{:S(2)}, u32[]{:S(2)}) collective-permute-start(bf16[16,4096]{1,0:T(8,128)(2,1)S(1)} %maximum_select_fusion.2), channel_id=1, source_target_pairs={{0,8},{1,9},{2,10},{3,11},{4,12},{5,13},{6,14},{7,15},{8,0},{9,1},... | collective-permute-start | bytes 393224 | tf_op jit(solution)/shard_map/ppermute | solution.py:20
  323.9 7.3 %copy-start.3 = (f32[16,512]{1,0:T(8,128)S(1)}, f32[16,512]{1,0:T(8,128)}, u32[]{:S(2)}) copy-start(f32[16,512]{1,0:T(8,128)} %reduce-scatter.2.cloned.1.call-done) | copy-start | bytes 98308
  323.9 12.5 %collective-permute-start.4 = (bf16[16,8192]{1,0:T(8,128)(2,1)S(1)}, bf16[16,8192]{1,0:T(8,128)(2,1)}, u32[]{:S(2)}, u32[]{:S(2)}) collective-permute-start(bf16[16,8192]{1,0:T(8,128)(2,1)S(1)} %maximum_select_fusion.1), channel_id=1, source_target_pairs={{0,16},{1,17},{2,18},{3,19},{4,20},{5,21},{6,22},{7,23},{8,24},{9,... | collective-permute-start | bytes 786440 | tf_op jit(solution)/shard_map/ppermute | solution.py:20
  331.2 7.2 %copy-start.2 = (f32[128,512]{1,0:T(8,128)}, f32[128,512]{1,0:T(8,128)S(1)}, u32[]{:S(2)}) copy-start(f32[128,512]{1,0:T(8,128)S(1)} %scatter_custom_fusion) | copy-start | bytes 786436
  332.1 6.3 %copy-start.1 = (f32[128,512]{1,0:T(8,128)}, f32[128,512]{1,0:T(8,128)S(1)}, u32[]{:S(2)}) copy-start(f32[128,512]{1,0:T(8,128)S(1)} %scatter_custom_fusion.1) | copy-start | bytes 786436
  333.0 5.4 %copy-start = (f32[128,512]{1,0:T(8,128)}, f32[128,512]{1,0:T(8,128)S(1)}, u32[]{:S(2)}) copy-start(f32[128,512]{1,0:T(8,128)S(1)} %scatter_custom_fusion.2) | copy-start | bytes 786436
Sparse Core Ops, SparseCore 0:
  126.3 139.2 reduce-scatter.1
